TPU v7x, 256 devices: a whole 4x4x8 slice. The times are simulated.
256 devices in a mesh: blk: 32 (over x, z), uly: 8 (over y, core).
Axes of the slice: x: 4, y: 4, z: 8, core: 2. Of those that a mesh axis runs over, the one named last changes fastest.
Arguments:
- tokens: bfloat16 [12288, 3072], P(('blk', 'uly')), may hold values from -6 to 6
- mod_shift: float32 [3072], replicated, may hold values from -3 to 3
- mod_scale: float32 [3072], replicated, may hold values from -2 to 6
- out_gate: float32 [3072], replicated, may hold values from 0.5 to 1.5
- w_qkv: bfloat16 [3072, 24, 384], P(None, 'uly'), may hold values from -0.109375 to 0.109375
- w_out: bfloat16 [3072, 3072], P('uly'), may hold values from -0.109375 to 0.109375
- tile_map: int32 [32], replicated, may hold values from 0 to 31, as said below
- window_corner: int32 [32, 2], replicated, may hold values from 0 to 5, as said below
Outputs:
- mixed: bfloat16 [12288, 3072], P(('blk', 'uly'))
Inputs may be any that keep to these rules, and one draw needn't show every extreme that they name: `tile_map`: A permutation of the tile positions; position j holds a grid tile whose number differs from j by at most 1. `window_corner`: each query tile's 3 x 3 window lies inside the grid and contains the grid tile that its own position holds.
All inputs are finite; a program needn't handle non-finite values.
Results may differ from a plain program's by a relative error of at most 0.02.
The roundings to bfloat16 on the way count: a program that leaves them out, or rounds other values in their place, can miss the bound.
Values may be sent and summed in bfloat16 or wider, within the bound.
A program may use at most 128 MiB of HBM per device.

v0:
```python
import jax
import jax.numpy as jnp
from jax import lax
from jax.sharding import PartitionSpec as P

TILE = 384
WIN = 3
GW = 4


def from_behind(block, axis, distance):
    devices = range(lax.axis_size(axis))
    route = [(i - distance, i) for i in devices if i - distance in devices]
    return lax.ppermute(block, axis, route)


def on_device(tokens, mod_shift, mod_scale, out_gate, w_qkv, w_out, tile_map, window_corner):
    values_in = tokens.astype(jnp.float32)
    mean_row = jnp.mean(values_in, axis=-1, keepdims=True)
    centred = values_in - mean_row
    variance = jnp.mean(centred * centred, axis=-1, keepdims=True)
    normed = (centred * lax.rsqrt(variance + 1e-06) * (1.0 + mod_scale) + mod_shift).astype(
        jnp.bfloat16
    )
    heads_dev = w_qkv.shape[1]
    head_dim = w_qkv.shape[2] // 3
    qkv = jnp.einsum(
        "td,dhe->the",
        lax.all_gather(normed, "uly", axis=0, tiled=True),
        w_qkv,
        preferred_element_type=jnp.float32,
    ).astype(jnp.bfloat16)
    group_rows = qkv.shape[0]
    tiles_here = group_rows // TILE
    all_tiles = tile_map.shape[0]
    queries = qkv[:, :, :head_dim]
    keyval = qkv[:, :, head_dim:]
    shard_idx = lax.axis_index("blk")
    n_blk = lax.axis_size("blk")
    first_tile = shard_idx * tiles_here
    query_corner = lax.dynamic_slice(window_corner, (first_tile, 0), (tiles_here, 2))
    softmax_factor = 1.0 / jnp.sqrt(jnp.float32(head_dim))

    def attend(running, kv_tile, key_tile, is_valid):
        safe_tile = jnp.clip(key_tile, 0, all_tiles - 1)
        key_grid = lax.dynamic_index_in_dim(tile_map, safe_tile, keepdims=False)
        row_gap = key_grid // GW - query_corner[:, 0]
        col_gap = key_grid % GW - query_corner[:, 1]
        inside = (row_gap >= 0) & (row_gap < WIN) & (col_gap >= 0) & (col_gap < WIN) & is_valid

        def compute(state):
            highest, total, accum = state
            row_ok = jnp.repeat(inside, TILE)[None, :, None]
            scores = (
                jnp.einsum(
                    "qhd,khd->hqk",
                    queries,
                    kv_tile[:, :, :head_dim],
                    preferred_element_type=jnp.float32,
                )
                * softmax_factor
            )
            scores = jnp.where(row_ok, scores, -1e30)
            new_high = jnp.maximum(highest, jnp.max(scores, axis=-1))
            probs = jnp.where(row_ok, jnp.exp(scores - new_high[:, :, None]), 0.0)
            factor = jnp.exp(highest - new_high)
            total = total * factor + jnp.sum(probs, axis=-1)
            weights = probs.astype(jnp.bfloat16)
            accum = accum * factor[:, :, None] + jnp.einsum(
                "hqk,khd->hqd",
                weights,
                kv_tile[:, :, head_dim:],
                preferred_element_type=jnp.float32,
            )
            return (new_high, total, accum)

        def keep(state):
            return state

        return lax.cond(jnp.any(inside), compute, keep, running)

    def attend_group(running, arrived, source):
        is_valid = (source >= 0) & (source < n_blk)
        running = attend(running, arrived, source * tiles_here + 0, is_valid)
        return running

    running = (
        jnp.full((heads_dev, group_rows), -1e30, jnp.float32),
        jnp.zeros((heads_dev, group_rows), jnp.float32),
        jnp.zeros((heads_dev, group_rows, head_dim), jnp.float32),
    )
    reach = min((2 * GW + 3 + tiles_here) // tiles_here, n_blk - 1)
    running = attend_group(running, keyval, shard_idx)
    for offset in range(-reach, reach + 1):
        if offset != 0:
            arrived = from_behind(keyval, "blk", offset)
            running = attend_group(running, arrived, shard_idx - offset)
    highest, total, accum = running
    attn = (accum / total[:, :, None]).astype(jnp.bfloat16)
    attn = jnp.transpose(attn, (1, 0, 2)).reshape(group_rows, heads_dev * head_dim)
    summed = lax.psum_scatter(
        jnp.dot(attn, w_out, preferred_element_type=jnp.float32).astype(jnp.bfloat16),
        "uly",
        scatter_dimension=0,
        tiled=True,
    ).astype(jnp.float32)
    return (out_gate * summed).astype(jnp.bfloat16)


def solution(mesh):
    in_specs = (
        P(("blk", "uly"), None),
        P(),
        P(),
        P(),
        P(None, "uly", None),
        P("uly", None),
        P(),
        P(),
    )
    out_specs = P(("blk", "uly"), None)
    return jax.shard_map(
        on_device, mesh=mesh, in_specs=in_specs, out_specs=out_specs, check_vma=False
    )
```

profile of v0, /device:TPU:4, one launch (start us, length us, event | category | flops | bytes accessed | tf_op | source)
XLA Modules:
  0.0 685.6 jit_solution(6186179026058369950)
XLA Ops:
  11.7 31.2 %all-gather.2.cloned.1.call-done = bf16[384,3072]{1,0:T(8,128)(2,1)} async-done(((bf16[48,3072]{1,0:T(8,128)(2,1)}), bf16[384,3072]{1,0:T(8,128)(2,1)}) %all-gather.2.cloned.1.call-update) | async-done | bytes 2359312 | tf_op jit(solution)/shard_map/all_gather | solution.py:29
  42.9 6.9 %fusion.378 = bf16[384,3,384]{2,0,1:T(8,128)(2,1)S(1)} fusion(bf16[3072,3,384]{2,0,1:T(8,128)(2,1)} %param.62, bf16[384,3072]{1,0:T(8,128)(2,1)} %all-gather.2.cloned.1.call-done), kind=kOutput, calls=%fused_computation.479 | convolution fusion | flops 2718351360 | bytes 10321920 | tf_op jit(solution)/shard_map/td,dhe->the/dot_general | solution.py:27
  51.6 7.6 %collective-permute-start = (bf16[384,3,256]{2,0,1:T(8,128)(2,1)}, bf16[384,3,256]{2,0,1:T(8,128)(2,1)}, u32[]{:S(2)}, u32[]{:S(2)}) collective-permute-start(bf16[384,3,256]{2,0,1:T(8,128)(2,1)} %slice.214), channel_id=1, source_target_pairs={{96,0},{104,8},{112,16},{120,24},{128,32},{136,40},{144,48},{152,5... | collective-permute-start | bytes 1769480 | tf_op jit(solution)/shard_map/ppermute | solution.py:14
  59.2 1.9 collective-permute-start.1
  61.2 1.9 collective-permute-start.2
  63.1 1.9 collective-permute-start.3
  65.0 1.9 collective-permute-start.4
  67.0 18.3 %collective-permute-done = bf16[384,3,256]{2,0,1:T(8,128)(2,1)} collective-permute-done((bf16[384,3,256]{2,0,1:T(8,128)(2,1)}, bf16[384,3,256]{2,0,1:T(8,128)(2,1)}, u32[]{:S(2)}, u32[]{:S(2)}) %collective-permute-start) | collective-permute-done | bytes 589856 | tf_op jit(solution)/shard_map/ppermute | solution.py:14
  85.3 6.3 collective-permute-start.5
  91.6 34.4 %collective-permute-done.1 = bf16[384,3,256]{2,0,1:T(8,128)(2,1)} collective-permute-done((bf16[384,3,256]{2,0,1:T(8,128)(2,1)}, bf16[384,3,256]{2,0,1:T(8,128)(2,1)}, u32[]{:S(2)}, u32[]{:S(2)}) %collective-permute-start.1) | collective-permute-done | bytes 589856 | tf_op jit(solution)/shard_map/ppermute | solution.py:14
  126.0 1.9 collective-permute-start.6
  127.9 23.2 %collective-permute-done.2 = bf16[384,3,256]{2,0,1:T(8,128)(2,1)} collective-permute-done((bf16[384,3,256]{2,0,1:T(8,128)(2,1)}, bf16[384,3,256]{2,0,1:T(8,128)(2,1)}, u32[]{:S(2)}, u32[]{:S(2)}) %collective-permute-start.2) | collective-permute-done | bytes 589856 | tf_op jit(solution)/shard_map/ppermute | solution.py:14
  151.1 1.9 collective-permute-start.7
  153.0 12.4 %collective-permute-done.3 = bf16[384,3,256]{2,0,1:T(8,128)(2,1)} collective-permute-done((bf16[384,3,256]{2,0,1:T(8,128)(2,1)}, bf16[384,3,256]{2,0,1:T(8,128)(2,1)}, u32[]{:S(2)}, u32[]{:S(2)}) %collective-permute-start.3) | collective-permute-done | bytes 589856 | tf_op jit(solution)/shard_map/ppermute | solution.py:14
  165.4 7.0 %collective-permute-start.8 = (bf16[384,3,256]{2,0,1:T(8,128)(2,1)}, bf16[384,3,256]{2,0,1:T(8,128)(2,1)}, u32[]{:S(2)}, u32[]{:S(2)}) collective-permute-start(bf16[384,3,256]{2,0,1:T(8,128)(2,1)} %slice.214), channel_id=1, source_target_pairs={{32,0},{40,8},{48,16},{56,24},{64,32},{72,40},{80,48},{88,56},{96,... | collective-permute-start | bytes 1769480 | tf_op jit(solution)/shard_map/ppermute | solution.py:14
  172.4 17.0 %collective-permute-start.9 = (bf16[384,3,256]{2,0,1:T(8,128)(2,1)}, bf16[384,3,256]{2,0,1:T(8,128)(2,1)}, u32[]{:S(2)}, u32[]{:S(2)}) collective-permute-start(bf16[384,3,256]{2,0,1:T(8,128)(2,1)} %slice.214), channel_id=1, source_target_pairs={{24,0},{32,8},{40,16},{48,24},{56,32},{64,40},{72,48},{80,56},{88,... | collective-permute-start | bytes 1769480 | tf_op jit(solution)/shard_map/ppermute | solution.py:14
  189.4 1.9 collective-permute-start.10
  191.4 2.5 collective-permute-start.11
  193.9 23.3 %collective-permute-done.7 = bf16[384,3,256]{2,0,1:T(8,128)(2,1)} collective-permute-done((bf16[384,3,256]{2,0,1:T(8,128)(2,1)}, bf16[384,3,256]{2,0,1:T(8,128)(2,1)}, u32[]{:S(2)}, u32[]{:S(2)}) %collective-permute-start.7) | collective-permute-done | bytes 589856 | tf_op jit(solution)/shard_map/ppermute | solution.py:14
  217.1 21.0 %collective-permute-start.12 = (bf16[384,3,256]{2,0,1:T(8,128)(2,1)}, bf16[384,3,256]{2,0,1:T(8,128)(2,1)}, u32[]{:S(2)}, u32[]{:S(2)}) collective-permute-start(bf16[384,3,256]{2,0,1:T(8,128)(2,1)} %slice.214), channel_id=1, source_target_pairs={{0,8},{8,16},{16,24},{24,32},{32,40},{40,48},{48,56},{56,64},{64,7... | collective-permute-start | bytes 1769480 | tf_op jit(solution)/shard_map/ppermute | solution.py:14
  238.1 12.1 %collective-permute-start.13 = (bf16[384,3,256]{2,0,1:T(8,128)(2,1)}, bf16[384,3,256]{2,0,1:T(8,128)(2,1)}, u32[]{:S(2)}, u32[]{:S(2)}) collective-permute-start(bf16[384,3,256]{2,0,1:T(8,128)(2,1)} %slice.214), channel_id=1, source_target_pairs={{0,16},{8,24},{16,32},{24,40},{32,48},{40,56},{48,64},{56,72},{64,... | collective-permute-start | bytes 1769480 | tf_op jit(solution)/shard_map/ppermute | solution.py:14
  250.2 21.8 %collective-permute-done.9 = bf16[384,3,256]{2,0,1:T(8,128)(2,1)} collective-permute-done((bf16[384,3,256]{2,0,1:T(8,128)(2,1)}, bf16[384,3,256]{2,0,1:T(8,128)(2,1)}, u32[]{:S(2)}, u32[]{:S(2)}) %collective-permute-start.9) | collective-permute-done | bytes 589856 | tf_op jit(solution)/shard_map/ppermute | solution.py:14
  272.0 27.5 %collective-permute-start.14 = (bf16[384,3,256]{2,0,1:T(8,128)(2,1)}, bf16[384,3,256]{2,0,1:T(8,128)(2,1)}, u32[]{:S(2)}, u32[]{:S(2)}) collective-permute-start(bf16[384,3,256]{2,0,1:T(8,128)(2,1)} %slice.214), channel_id=1, source_target_pairs={{0,24},{8,32},{16,40},{24,48},{32,56},{40,64},{48,72},{56,80},{64,... | collective-permute-start | bytes 1769480 | tf_op jit(solution)/shard_map/ppermute | solution.py:14
  299.5 64.9 %collective-permute-start.15 = (bf16[384,3,256]{2,0,1:T(8,128)(2,1)}, bf16[384,3,256]{2,0,1:T(8,128)(2,1)}, u32[]{:S(2)}, u32[]{:S(2)}) collective-permute-start(bf16[384,3,256]{2,0,1:T(8,128)(2,1)} %slice.214), channel_id=1, source_target_pairs={{0,32},{8,40},{16,48},{24,56},{32,64},{40,72},{48,80},{56,88},{64,... | collective-permute-start | bytes 1769480 | tf_op jit(solution)/shard_map/ppermute | solution.py:14
  364.4 11.6 %collective-permute-start.16 = (bf16[384,3,256]{2,0,1:T(8,128)(2,1)}, bf16[384,3,256]{2,0,1:T(8,128)(2,1)}, u32[]{:S(2)}, u32[]{:S(2)}) collective-permute-start(bf16[384,3,256]{2,0,1:T(8,128)(2,1)} %slice.214), channel_id=1, source_target_pairs={{0,40},{8,48},{16,56},{24,64},{32,72},{40,80},{48,88},{56,96},{64,... | collective-permute-start | bytes 1769480 | tf_op jit(solution)/shard_map/ppermute | solution.py:14
  376.0 1.9 collective-permute-start.17
  378.0 1.9 collective-permute-start.18
  379.9 1.9 collective-permute-start.19
  381.9 7.5 %collective-permute-done.15 = bf16[384,3,256]{2,0,1:T(8,128)(2,1)} collective-permute-done((bf16[384,3,256]{2,0,1:T(8,128)(2,1)}, bf16[384,3,256]{2,0,1:T(8,128)(2,1)}, u32[]{:S(2)}, u32[]{:S(2)}) %collective-permute-start.15) | collective-permute-done | bytes 589856 | tf_op jit(solution)/shard_map/ppermute | solution.py:14
  389.3 1.9 collective-permute-start.20
  391.2 26.1 %collective-permute-done.16 = bf16[384,3,256]{2,0,1:T(8,128)(2,1)} collective-permute-done((bf16[384,3,256]{2,0,1:T(8,128)(2,1)}, bf16[384,3,256]{2,0,1:T(8,128)(2,1)}, u32[]{:S(2)}, u32[]{:S(2)}) %collective-permute-start.16) | collective-permute-done | bytes 589856 | tf_op jit(solution)/shard_map/ppermute | solution.py:14
  417.3 13.9 %collective-permute-start.21 = (bf16[384,3,256]{2,0,1:T(8,128)(2,1)}, bf16[384,3,256]{2,0,1:T(8,128)(2,1)}, u32[]{:S(2)}, u32[]{:S(2)}) collective-permute-start(bf16[384,3,256]{2,0,1:T(8,128)(2,1)} %slice.214), channel_id=1, source_target_pairs={{0,80},{8,88},{16,96},{24,104},{32,112},{40,120},{48,128},{56,136}... | collective-permute-start | bytes 1769480 | tf_op jit(solution)/shard_map/ppermute | solution.py:14
  431.3 12.6 %collective-permute-done.17 = bf16[384,3,256]{2,0,1:T(8,128)(2,1)} collective-permute-done((bf16[384,3,256]{2,0,1:T(8,128)(2,1)}, bf16[384,3,256]{2,0,1:T(8,128)(2,1)}, u32[]{:S(2)}, u32[]{:S(2)}) %collective-permute-start.17) | collective-permute-done | bytes 589856 | tf_op jit(solution)/shard_map/ppermute | solution.py:14
  443.8 1.9 collective-permute-start.22
  445.8 30.3 %collective-permute-done.18 = bf16[384,3,256]{2,0,1:T(8,128)(2,1)} collective-permute-done((bf16[384,3,256]{2,0,1:T(8,128)(2,1)}, bf16[384,3,256]{2,0,1:T(8,128)(2,1)}, u32[]{:S(2)}, u32[]{:S(2)}) %collective-permute-start.18) | collective-permute-done | bytes 589856 | tf_op jit(solution)/shard_map/ppermute | solution.py:14
  476.1 1.9 collective-permute-start.23
  573.9 5.5 conditional.25
  579.7 8.1 %conditional.34 = ((f32[3,384]{1,0:T(4,128)}, f32[3,384]{1,0:T(4,128)S(1)}, f32[3,384,128]{2,1,0:T(8,128)S(1)})) conditional(s32[]{:T(128)} %bitcast.106, (f32[3,384]{1,0:T(4,128)}, f32[3,384]{1,0:T(4,128)S(1)}, f32[3,384,128]{2,1,0:T(8,128)S(1)}) %get-tuple-element.1021, (pred[1]{0:T(512)(128)(4,1)}, bf16[384,3,256]{2,0,1:T(8,128)(2,1)}, ...), branch_computations={%region_38.39_spmd, %region_39.42_spmd} | conditional | flops 232540416 | bytes 7447585 | solution.py:80
  587.8 5.6 conditional.35
  593.4 6.3 conditional.37
  599.8 5.6 conditional.39
  605.4 5.6 conditional.40
  611.0 6.0 conditional.41
  617.0 5.6 conditional.43
  622.7 5.6 conditional.44
  628.3 5.6 conditional.45
  634.5 2.8 convolution_convert_fusion
  637.4 39.5 %reduce-scatter.2.cloned.1.call-done = bf16[48,3072]{1,0:T(8,128)(2,1)} async-done(((bf16[384,3072]{1,0:T(8,128)(2,1)}), bf16[48,3072]{1,0:T(8,128)(2,1)}) %reduce-scatter.2.cloned.1.call-update) | async-done | bytes 294928 | tf_op jit(solution)/shard_map/reduce_scatter | solution.py:101
  (110 shorter events, 63.6 us)
Async XLA Ops:
  6.5 627.9 %copy-start = (bf16[384,3072]{1,0:T(8,128)(2,1)S(1)}, bf16[384,3072]{1,0:T(8,128)(2,1)}, u32[]{:S(2)}) copy-start(bf16[384,3072]{1,0:T(8,128)(2,1)} %param.63) | copy-start | bytes 7077892
  6.5 36.4 %all-gather.2.cloned.1.call-start = ((), (), s32[]{:S(2)}) async-start(), calls=%async_computation.1 | async-start | bytes 2654208 | tf_op jit(solution)/shard_map/all_gather | solution.py:29
  11.6 466.4 %copy-start.2 = (s32[32]{0:T(128)S(1)}, s32[32]{0:T(128)}, u32[]{:S(2)}) copy-start(s32[32]{0:T(128)} %param.64) | copy-start | bytes 388
  11.6 469.6 %copy-start.4 = (s32[32,2]{0,1:T(2,128)S(1)}, s32[32,2]{0,1:T(2,128)}, u32[]{:S(2)}) copy-start(s32[32,2]{0,1:T(2,128)} %param.65) | copy-start | bytes 772
  11.6 665.2 %reduce-scatter.2.cloned.1.call-start = ((), (), s32[]{:S(2)}) async-start(), calls=%async_computation.2 | async-start | bytes 2654208 | tf_op jit(solution)/shard_map/reduce_scatter | solution.py:101
  49.8 0.9 copy-start.1
  51.6 33.7 %collective-permute-start = (bf16[384,3,256]{2,0,1:T(8,128)(2,1)}, bf16[384,3,256]{2,0,1:T(8,128)(2,1)}, u32[]{:S(2)}, u32[]{:S(2)}) collective-permute-start(bf16[384,3,256]{2,0,1:T(8,128)(2,1)} %slice.214), channel_id=1, source_target_pairs={{96,0},{104,8},{112,16},{120,24},{128,32},{136,40},{144,48},{152,5... | collective-permute-start | bytes 1769480 | tf_op jit(solution)/shard_map/ppermute | solution.py:14
  59.2 66.8 %collective-permute-start.1 = (bf16[384,3,256]{2,0,1:T(8,128)(2,1)}, bf16[384,3,256]{2,0,1:T(8,128)(2,1)}, u32[]{:S(2)}, u32[]{:S(2)}) collective-permute-start(bf16[384,3,256]{2,0,1:T(8,128)(2,1)} %slice.214), channel_id=1, source_target_pairs={{88,0},{96,8},{104,16},{112,24},{120,32},{128,40},{136,48},{144,56... | collective-permute-start | bytes 1769480 | tf_op jit(solution)/shard_map/ppermute | solution.py:14
  61.2 90.0 %collective-permute-start.2 = (bf16[384,3,256]{2,0,1:T(8,128)(2,1)}, bf16[384,3,256]{2,0,1:T(8,128)(2,1)}, u32[]{:S(2)}, u32[]{:S(2)}) collective-permute-start(bf16[384,3,256]{2,0,1:T(8,128)(2,1)} %slice.214), channel_id=1, source_target_pairs={{80,0},{88,8},{96,16},{104,24},{112,32},{120,40},{128,48},{136,56}... | collective-permute-start | bytes 1769480 | tf_op jit(solution)/shard_map/ppermute | solution.py:14
  63.1 102.3 %collective-permute-start.3 = (bf16[384,3,256]{2,0,1:T(8,128)(2,1)}, bf16[384,3,256]{2,0,1:T(8,128)(2,1)}, u32[]{:S(2)}, u32[]{:S(2)}) collective-permute-start(bf16[384,3,256]{2,0,1:T(8,128)(2,1)} %slice.214), channel_id=1, source_target_pairs={{72,0},{80,8},{88,16},{96,24},{104,32},{112,40},{120,48},{128,56},... | collective-permute-start | bytes 1769480 | tf_op jit(solution)/shard_map/ppermute | solution.py:14
  65.0 107.4 %collective-permute-start.4 = (bf16[384,3,256]{2,0,1:T(8,128)(2,1)}, bf16[384,3,256]{2,0,1:T(8,128)(2,1)}, u32[]{:S(2)}, u32[]{:S(2)}) collective-permute-start(bf16[384,3,256]{2,0,1:T(8,128)(2,1)} %slice.214), channel_id=1, source_target_pairs={{64,0},{72,8},{80,16},{88,24},{96,32},{104,40},{112,48},{120,56},{... | collective-permute-start | bytes 1769480 | tf_op jit(solution)/shard_map/ppermute | solution.py:14
  85.3 104.2 %collective-permute-start.5 = (bf16[384,3,256]{2,0,1:T(8,128)(2,1)}, bf16[384,3,256]{2,0,1:T(8,128)(2,1)}, u32[]{:S(2)}, u32[]{:S(2)}) collective-permute-start(bf16[384,3,256]{2,0,1:T(8,128)(2,1)} %slice.214), channel_id=1, source_target_pairs={{56,0},{64,8},{72,16},{80,24},{88,32},{96,40},{104,48},{112,56},{1... | collective-permute-start | bytes 1769480 | tf_op jit(solution)/shard_map/ppermute | solution.py:14
  126.0 65.4 %collective-permute-start.6 = (bf16[384,3,256]{2,0,1:T(8,128)(2,1)}, bf16[384,3,256]{2,0,1:T(8,128)(2,1)}, u32[]{:S(2)}, u32[]{:S(2)}) collective-permute-start(bf16[384,3,256]{2,0,1:T(8,128)(2,1)} %slice.214), channel_id=1, source_target_pairs={{48,0},{56,8},{64,16},{72,24},{80,32},{88,40},{96,48},{104,56},{11... | collective-permute-start | bytes 1769480 | tf_op jit(solution)/shard_map/ppermute | solution.py:14
  151.1 66.0 %collective-permute-start.7 = (bf16[384,3,256]{2,0,1:T(8,128)(2,1)}, bf16[384,3,256]{2,0,1:T(8,128)(2,1)}, u32[]{:S(2)}, u32[]{:S(2)}) collective-permute-start(bf16[384,3,256]{2,0,1:T(8,128)(2,1)} %slice.214), channel_id=1, source_target_pairs={{40,0},{48,8},{56,16},{64,24},{72,32},{80,40},{88,48},{96,56},{104... | collective-permute-start | bytes 1769480 | tf_op jit(solution)/shard_map/ppermute | solution.py:14
  165.4 72.7 %collective-permute-start.8 = (bf16[384,3,256]{2,0,1:T(8,128)(2,1)}, bf16[384,3,256]{2,0,1:T(8,128)(2,1)}, u32[]{:S(2)}, u32[]{:S(2)}) collective-permute-start(bf16[384,3,256]{2,0,1:T(8,128)(2,1)} %slice.214), channel_id=1, source_target_pairs={{32,0},{40,8},{48,16},{56,24},{64,32},{72,40},{80,48},{88,56},{96,... | collective-permute-start | bytes 1769480 | tf_op jit(solution)/shard_map/ppermute | solution.py:14
  172.4 99.6 %collective-permute-start.9 = (bf16[384,3,256]{2,0,1:T(8,128)(2,1)}, bf16[384,3,256]{2,0,1:T(8,128)(2,1)}, u32[]{:S(2)}, u32[]{:S(2)}) collective-permute-start(bf16[384,3,256]{2,0,1:T(8,128)(2,1)} %slice.214), channel_id=1, source_target_pairs={{24,0},{32,8},{40,16},{48,24},{56,32},{64,40},{72,48},{80,56},{88,... | collective-permute-start | bytes 1769480 | tf_op jit(solution)/shard_map/ppermute | solution.py:14
  189.4 110.1 %collective-permute-start.10 = (bf16[384,3,256]{2,0,1:T(8,128)(2,1)}, bf16[384,3,256]{2,0,1:T(8,128)(2,1)}, u32[]{:S(2)}, u32[]{:S(2)}) collective-permute-start(bf16[384,3,256]{2,0,1:T(8,128)(2,1)} %slice.214), channel_id=1, source_target_pairs={{16,0},{24,8},{32,16},{40,24},{48,32},{56,40},{64,48},{72,56},{80,... | collective-permute-start | bytes 1769480 | tf_op jit(solution)/shard_map/ppermute | solution.py:14
  191.4 173.0 %collective-permute-start.11 = (bf16[384,3,256]{2,0,1:T(8,128)(2,1)}, bf16[384,3,256]{2,0,1:T(8,128)(2,1)}, u32[]{:S(2)}, u32[]{:S(2)}) collective-permute-start(bf16[384,3,256]{2,0,1:T(8,128)(2,1)} %slice.214), channel_id=1, source_target_pairs={{8,0},{16,8},{24,16},{32,24},{40,32},{48,40},{56,48},{64,56},{72,6... | collective-permute-start | bytes 1769480 | tf_op jit(solution)/shard_map/ppermute | solution.py:14
  217.1 158.9 %collective-permute-start.12 = (bf16[384,3,256]{2,0,1:T(8,128)(2,1)}, bf16[384,3,256]{2,0,1:T(8,128)(2,1)}, u32[]{:S(2)}, u32[]{:S(2)}) collective-permute-start(bf16[384,3,256]{2,0,1:T(8,128)(2,1)} %slice.214), channel_id=1, source_target_pairs={{0,8},{8,16},{16,24},{24,32},{32,40},{40,48},{48,56},{56,64},{64,7... | collective-permute-start | bytes 1769480 | tf_op jit(solution)/shard_map/ppermute | solution.py:14
  238.1 139.8 %collective-permute-start.13 = (bf16[384,3,256]{2,0,1:T(8,128)(2,1)}, bf16[384,3,256]{2,0,1:T(8,128)(2,1)}, u32[]{:S(2)}, u32[]{:S(2)}) collective-permute-start(bf16[384,3,256]{2,0,1:T(8,128)(2,1)} %slice.214), channel_id=1, source_target_pairs={{0,16},{8,24},{16,32},{24,40},{32,48},{40,56},{48,64},{56,72},{64,... | collective-permute-start | bytes 1769480 | tf_op jit(solution)/shard_map/ppermute | solution.py:14
  272.0 107.9 %collective-permute-start.14 = (bf16[384,3,256]{2,0,1:T(8,128)(2,1)}, bf16[384,3,256]{2,0,1:T(8,128)(2,1)}, u32[]{:S(2)}, u32[]{:S(2)}) collective-permute-start(bf16[384,3,256]{2,0,1:T(8,128)(2,1)} %slice.214), channel_id=1, source_target_pairs={{0,24},{8,32},{16,40},{24,48},{32,56},{40,64},{48,72},{56,80},{64,... | collective-permute-start | bytes 1769480 | tf_op jit(solution)/shard_map/ppermute | solution.py:14
  299.5 89.8 %collective-permute-start.15 = (bf16[384,3,256]{2,0,1:T(8,128)(2,1)}, bf16[384,3,256]{2,0,1:T(8,128)(2,1)}, u32[]{:S(2)}, u32[]{:S(2)}) collective-permute-start(bf16[384,3,256]{2,0,1:T(8,128)(2,1)} %slice.214), channel_id=1, source_target_pairs={{0,32},{8,40},{16,48},{24,56},{32,64},{40,72},{48,80},{56,88},{64,... | collective-permute-start | bytes 1769480 | tf_op jit(solution)/shard_map/ppermute | solution.py:14
  364.4 52.9 %collective-permute-start.16 = (bf16[384,3,256]{2,0,1:T(8,128)(2,1)}, bf16[384,3,256]{2,0,1:T(8,128)(2,1)}, u32[]{:S(2)}, u32[]{:S(2)}) collective-permute-start(bf16[384,3,256]{2,0,1:T(8,128)(2,1)} %slice.214), channel_id=1, source_target_pairs={{0,40},{8,48},{16,56},{24,64},{32,72},{40,80},{48,88},{56,96},{64,... | collective-permute-start | bytes 1769480 | tf_op jit(solution)/shard_map/ppermute | solution.py:14
  376.0 67.8 %collective-permute-start.17 = (bf16[384,3,256]{2,0,1:T(8,128)(2,1)}, bf16[384,3,256]{2,0,1:T(8,128)(2,1)}, u32[]{:S(2)}, u32[]{:S(2)}) collective-permute-start(bf16[384,3,256]{2,0,1:T(8,128)(2,1)} %slice.214), channel_id=1, source_target_pairs={{0,48},{8,56},{16,64},{24,72},{32,80},{40,88},{48,96},{56,104},{64... | collective-permute-start | bytes 1769480 | tf_op jit(solution)/shard_map/ppermute | solution.py:14
  378.0 98.1 %collective-permute-start.18 = (bf16[384,3,256]{2,0,1:T(8,128)(2,1)}, bf16[384,3,256]{2,0,1:T(8,128)(2,1)}, u32[]{:S(2)}, u32[]{:S(2)}) collective-permute-start(bf16[384,3,256]{2,0,1:T(8,128)(2,1)} %slice.214), channel_id=1, source_target_pairs={{0,56},{8,64},{16,72},{24,80},{32,88},{40,96},{48,104},{56,112},{6... | collective-permute-start | bytes 1769480 | tf_op jit(solution)/shard_map/ppermute | solution.py:14
  379.9 248.4 %collective-permute-start.19 = (bf16[384,3,256]{2,0,1:T(8,128)(2,1)}, bf16[384,3,256]{2,0,1:T(8,128)(2,1)}, u32[]{:S(2)}, u32[]{:S(2)}) collective-permute-start(bf16[384,3,256]{2,0,1:T(8,128)(2,1)} %slice.214), channel_id=1, source_target_pairs={{0,64},{8,72},{16,80},{24,88},{32,96},{40,104},{48,112},{56,120},{... | collective-permute-start | bytes 1769480 | tf_op jit(solution)/shard_map/ppermute | solution.py:14
  389.3 244.6 %collective-permute-start.20 = (bf16[384,3,256]{2,0,1:T(8,128)(2,1)}, bf16[384,3,256]{2,0,1:T(8,128)(2,1)}, u32[]{:S(2)}, u32[]{:S(2)}) collective-permute-start(bf16[384,3,256]{2,0,1:T(8,128)(2,1)} %slice.214), channel_id=1, source_target_pairs={{0,72},{8,80},{16,88},{24,96},{32,104},{40,112},{48,120},{56,128},... | collective-permute-start | bytes 1769480 | tf_op jit(solution)/shard_map/ppermute | solution.py:14
  417.3 216.6 %collective-permute-start.21 = (bf16[384,3,256]{2,0,1:T(8,128)(2,1)}, bf16[384,3,256]{2,0,1:T(8,128)(2,1)}, u32[]{:S(2)}, u32[]{:S(2)}) collective-permute-start(bf16[384,3,256]{2,0,1:T(8,128)(2,1)} %slice.214), channel_id=1, source_target_pairs={{0,80},{8,88},{16,96},{24,104},{32,112},{40,120},{48,128},{56,136}... | collective-permute-start | bytes 1769480 | tf_op jit(solution)/shard_map/ppermute | solution.py:14
  443.8 190.1 %collective-permute-start.22 = (bf16[384,3,256]{2,0,1:T(8,128)(2,1)}, bf16[384,3,256]{2,0,1:T(8,128)(2,1)}, u32[]{:S(2)}, u32[]{:S(2)}) collective-permute-start(bf16[384,3,256]{2,0,1:T(8,128)(2,1)} %slice.214), channel_id=1, source_target_pairs={{0,88},{8,96},{16,104},{24,112},{32,120},{40,128},{48,136},{56,144... | collective-permute-start | bytes 1769480 | tf_op jit(solution)/shard_map/ppermute | solution.py:14
  476.1 158.1 %collective-permute-start.23 = (bf16[384,3,256]{2,0,1:T(8,128)(2,1)}, bf16[384,3,256]{2,0,1:T(8,128)(2,1)}, u32[]{:S(2)}, u32[]{:S(2)}) collective-permute-start(bf16[384,3,256]{2,0,1:T(8,128)(2,1)} %slice.214), channel_id=1, source_target_pairs={{0,96},{8,104},{16,112},{24,120},{32,128},{40,136},{48,144},{56,15... | collective-permute-start | bytes 1769480 | tf_op jit(solution)/shard_map/ppermute | solution.py:14
  637.3 39.5 %copy-start.3 = (f32[3072]{0:T(1024)S(1)}, f32[3072]{0:T(1024)}, u32[]{:S(2)}) copy-start(f32[3072]{0:T(1024)} %param.61) | copy-start | bytes 36868
Sparse Core Ops, SparseCore 0:
  11.7 31.0 all-gather.1
  637.5 39.3 reduce-scatter.1
where the time goes:
time: 697 us; the launch traced here: 686 us
  waiting for transfers between devices  281 us (40%)
  starting transfers between devices  216 us (31%)
  between operations  107 us (15%)
  matrix products  38.1 us (5%)
  other arithmetic  25.2 us (4%)
  local copies, waits for them, and re-layouts  9.26 us (1%)
  loops' own time  9.18 us (1%)
    ppermute x24, starting transfers between devices, from_behind(): return lax.ppermute(block, axis, route)  216 us
    ppermute x24, waiting for transfers between devices, from_behind(): return lax.ppermute(block, axis, route)  210 us
    reduce_scatter x1, waiting for transfers between devices, on_device(): lax.psum_scatter(jnp.dot(attn, w_out, preferred_element_type=jnp.float32)...  39.5 us
    all_gather x1, waiting for transfers between devices, on_device(): lax.all_gather(normed, 'uly', axis=0, tiled=True)  31.2 us
    dot_general x9, matrix products, compute(): jnp.einsum('hqk,khd->hqd', weights, kv_tile[:, :, head_dim:], preferred_e...  15.8 us
  transfers between devices with their start and end apart: 26, of which 12 were waited for; matrix products, arithmetic and copies ran while one was open for 8% of the time, Pallas kernels for 0%

commit v1 on v0

--- a/solution.py
+++ b/solution.py
@@ -26,7 +26,9 @@
     head_dim = w_qkv.shape[2] // 3
     qkv = jnp.einsum(
         "td,dhe->the",
-        lax.all_gather(normed, "uly", axis=0, tiled=True),
+        jnp.concatenate(
+            jax.lax.all_to_all(jnp.stack(jax.lax.psum(1, "uly") * [normed]), "uly", 0, 0), axis=0
+        ),
         w_qkv,
         preferred_element_type=jnp.float32,
     ).astype(jnp.bfloat16)

time: 697 us -> 670 us (0.961)
  starting transfers between devices: 216 us -> 168 us
  blocking collectives: 0 us -> 34.9 us
  waiting for transfers between devices: 281 us -> 273 us
    ppermute x24, starting transfers between devices: 216 us -> 168 us  [from_behind(): return lax.ppermute(block, axis, route)]
    all_to_all x0 -> x1, blocking collectives: none -> 34.9 us  [on_device(): jax.lax.all_to_all(jnp.stack(jax.lax.psum(1, 'uly') * [normed]), 'uly', 0...]
    all_gather x1 -> x0, waiting for transfers between devices: 31.2 us -> none  [on_device(): lax.all_gather(normed, 'uly', axis=0, tiled=True)]
    reduce_scatter x1, waiting for transfers between devices: 39.5 us -> 59.5 us  [on_device(): lax.psum_scatter(jnp.dot(attn, w_out, preferred_element_type=jnp.float32)...]
  transfers between devices with their start and end apart: 26 -> 25, of which waited for: 12 -> 11; matrix products, arithmetic and copies ran while one was open for 8% -> 8% of each run, Pallas kernels for 0% -> 0%
where the time goes in v1:
time: 670 us; the launch traced here: 659 us
  waiting for transfers between devices  273 us (41%)
  starting transfers between devices  168 us (25%)
  between operations  106 us (16%)
  blocking collectives  34.9 us (5%)
  matrix products  34.4 us (5%)
  other arithmetic  24.5 us (4%)
  local copies, waits for them, and re-layouts  9.49 us (1%)
  loops' own time  9.06 us (1%)
    ppermute x24, waiting for transfers between devices, from_behind(): return lax.ppermute(block, axis, route)  213 us
    ppermute x24, starting transfers between devices, from_behind(): return lax.ppermute(block, axis, route)  168 us
    reduce_scatter x1, waiting for transfers between devices, on_device(): lax.psum_scatter(jnp.dot(attn, w_out, preferred_element_type=jnp.float32)...  59.5 us
    all_to_all x1, blocking collectives, on_device(): jax.lax.all_to_all(jnp.stack(jax.lax.psum(1, 'uly') * [normed]), 'uly', 0...  34.9 us
    dot_general x9, matrix products, compute(): jnp.einsum('hqk,khd->hqd', weights, kv_tile[:, :, head_dim:], preferred_e...  15.8 us
  transfers between devices with their start and end apart: 25, of which 11 were waited for; matrix products, arithmetic and copies ran while one was open for 8% of the time, Pallas kernels for 0%

profile of v1, /device:TPU:4, one launch (start us, length us, event | category | flops | bytes accessed | tf_op | source)
XLA Modules:
  0.0 659.0 jit_solution(14448534223743909291)
XLA Ops:
  11.2 34.9 %all_to_all.5 = bf16[8,48,3072]{2,1,0:T(8,128)(2,1)S(1)} all-to-all(bf16[8,48,3072]{2,1,0:T(8,128)(2,1)S(1)} %stack.2), channel_id=1, replica_groups=mesh['blk'=32,'uly'=8] {'uly'}, dimensions={0} | all-to-all | bytes 4718592 | tf_op jit(solution)/shard_map/all_to_all | solution.py:30
  46.1 3.2 convolution_convert_fusion.1
  51.1 9.0 %collective-permute-start = (bf16[384,3,256]{2,0,1:T(8,128)(2,1)}, bf16[384,3,256]{2,0,1:T(8,128)(2,1)}, u32[]{:S(2)}, u32[]{:S(2)}) collective-permute-start(bf16[384,3,256]{2,0,1:T(8,128)(2,1)} %slice.214), channel_id=1, source_target_pairs={{96,0},{104,8},{112,16},{120,24},{128,32},{136,40},{144,48},{152,5... | collective-permute-start | bytes 1769480 | tf_op jit(solution)/shard_map/ppermute | solution.py:14
  60.2 1.9 collective-permute-start.1
  62.1 1.9 collective-permute-start.2
  64.0 1.9 collective-permute-start.3
  65.9 1.9 collective-permute-start.4
  67.9 17.7 %collective-permute-done = bf16[384,3,256]{2,0,1:T(8,128)(2,1)} collective-permute-done((bf16[384,3,256]{2,0,1:T(8,128)(2,1)}, bf16[384,3,256]{2,0,1:T(8,128)(2,1)}, u32[]{:S(2)}, u32[]{:S(2)}) %collective-permute-start) | collective-permute-done | bytes 589856 | tf_op jit(solution)/shard_map/ppermute | solution.py:14
  85.6 7.6 %collective-permute-start.5 = (bf16[384,3,256]{2,0,1:T(8,128)(2,1)}, bf16[384,3,256]{2,0,1:T(8,128)(2,1)}, u32[]{:S(2)}, u32[]{:S(2)}) collective-permute-start(bf16[384,3,256]{2,0,1:T(8,128)(2,1)} %slice.214), channel_id=1, source_target_pairs={{56,0},{64,8},{72,16},{80,24},{88,32},{96,40},{104,48},{112,56},{1... | collective-permute-start | bytes 1769480 | tf_op jit(solution)/shard_map/ppermute | solution.py:14
  93.2 33.0 %collective-permute-done.1 = bf16[384,3,256]{2,0,1:T(8,128)(2,1)} collective-permute-done((bf16[384,3,256]{2,0,1:T(8,128)(2,1)}, bf16[384,3,256]{2,0,1:T(8,128)(2,1)}, u32[]{:S(2)}, u32[]{:S(2)}) %collective-permute-start.1) | collective-permute-done | bytes 589856 | tf_op jit(solution)/shard_map/ppermute | solution.py:14
  126.1 1.9 collective-permute-start.6
  128.1 21.5 %collective-permute-done.2 = bf16[384,3,256]{2,0,1:T(8,128)(2,1)} collective-permute-done((bf16[384,3,256]{2,0,1:T(8,128)(2,1)}, bf16[384,3,256]{2,0,1:T(8,128)(2,1)}, u32[]{:S(2)}, u32[]{:S(2)}) %collective-permute-start.2) | collective-permute-done | bytes 589856 | tf_op jit(solution)/shard_map/ppermute | solution.py:14
  149.6 1.9 collective-permute-start.7
  151.5 13.0 %collective-permute-done.3 = bf16[384,3,256]{2,0,1:T(8,128)(2,1)} collective-permute-done((bf16[384,3,256]{2,0,1:T(8,128)(2,1)}, bf16[384,3,256]{2,0,1:T(8,128)(2,1)}, u32[]{:S(2)}, u32[]{:S(2)}) %collective-permute-start.3) | collective-permute-done | bytes 589856 | tf_op jit(solution)/shard_map/ppermute | solution.py:14
  164.5 5.3 collective-permute-start.8
  169.8 44.7 %collective-permute-start.9 = (bf16[384,3,256]{2,0,1:T(8,128)(2,1)}, bf16[384,3,256]{2,0,1:T(8,128)(2,1)}, u32[]{:S(2)}, u32[]{:S(2)}) collective-permute-start(bf16[384,3,256]{2,0,1:T(8,128)(2,1)} %slice.214), channel_id=1, source_target_pairs={{24,0},{32,8},{40,16},{48,24},{56,32},{64,40},{72,48},{80,56},{88,... | collective-permute-start | bytes 1769480 | tf_op jit(solution)/shard_map/ppermute | solution.py:14
  214.5 1.9 collective-permute-start.10
  216.5 2.5 collective-permute-start.11
  219.0 8.9 %collective-permute-start.12 = (bf16[384,3,256]{2,0,1:T(8,128)(2,1)}, bf16[384,3,256]{2,0,1:T(8,128)(2,1)}, u32[]{:S(2)}, u32[]{:S(2)}) collective-permute-start(bf16[384,3,256]{2,0,1:T(8,128)(2,1)} %slice.214), channel_id=1, source_target_pairs={{0,8},{8,16},{16,24},{24,32},{32,40},{40,48},{48,56},{56,64},{64,7... | collective-permute-start | bytes 1769480 | tf_op jit(solution)/shard_map/ppermute | solution.py:14
  227.9 5.8 collective-permute-done.8
  233.6 9.2 %collective-permute-start.13 = (bf16[384,3,256]{2,0,1:T(8,128)(2,1)}, bf16[384,3,256]{2,0,1:T(8,128)(2,1)}, u32[]{:S(2)}, u32[]{:S(2)}) collective-permute-start(bf16[384,3,256]{2,0,1:T(8,128)(2,1)} %slice.214), channel_id=1, source_target_pairs={{0,16},{8,24},{16,32},{24,40},{32,48},{40,56},{48,64},{56,72},{64,... | collective-permute-start | bytes 1769480 | tf_op jit(solution)/shard_map/ppermute | solution.py:14
  242.8 13.9 %collective-permute-done.9 = bf16[384,3,256]{2,0,1:T(8,128)(2,1)} collective-permute-done((bf16[384,3,256]{2,0,1:T(8,128)(2,1)}, bf16[384,3,256]{2,0,1:T(8,128)(2,1)}, u32[]{:S(2)}, u32[]{:S(2)}) %collective-permute-start.9) | collective-permute-done | bytes 589856 | tf_op jit(solution)/shard_map/ppermute | solution.py:14
  256.8 8.5 %collective-permute-start.14 = (bf16[384,3,256]{2,0,1:T(8,128)(2,1)}, bf16[384,3,256]{2,0,1:T(8,128)(2,1)}, u32[]{:S(2)}, u32[]{:S(2)}) collective-permute-start(bf16[384,3,256]{2,0,1:T(8,128)(2,1)} %slice.214), channel_id=1, source_target_pairs={{0,24},{8,32},{16,40},{24,48},{32,56},{40,64},{48,72},{56,80},{64,... | collective-permute-start | bytes 1769480 | tf_op jit(solution)/shard_map/ppermute | solution.py:14
  265.3 19.2 %collective-permute-done.10 = bf16[384,3,256]{2,0,1:T(8,128)(2,1)} collective-permute-done((bf16[384,3,256]{2,0,1:T(8,128)(2,1)}, bf16[384,3,256]{2,0,1:T(8,128)(2,1)}, u32[]{:S(2)}, u32[]{:S(2)}) %collective-permute-start.10) | collective-permute-done | bytes 589856 | tf_op jit(solution)/shard_map/ppermute | solution.py:14
  284.5 4.6 collective-permute-start.15
  289.1 39.6 %collective-permute-done.11 = bf16[384,3,256]{2,0,1:T(8,128)(2,1)} collective-permute-done((bf16[384,3,256]{2,0,1:T(8,128)(2,1)}, bf16[384,3,256]{2,0,1:T(8,128)(2,1)}, u32[]{:S(2)}, u32[]{:S(2)}) %collective-permute-start.11) | collective-permute-done | bytes 589856 | tf_op jit(solution)/shard_map/ppermute | solution.py:14
  328.6 1.9 collective-permute-start.16
  330.6 30.7 %collective-permute-start.17 = (bf16[384,3,256]{2,0,1:T(8,128)(2,1)}, bf16[384,3,256]{2,0,1:T(8,128)(2,1)}, u32[]{:S(2)}, u32[]{:S(2)}) collective-permute-start(bf16[384,3,256]{2,0,1:T(8,128)(2,1)} %slice.214), channel_id=1, source_target_pairs={{0,48},{8,56},{16,64},{24,72},{32,80},{40,88},{48,96},{56,104},{64... | collective-permute-start | bytes 1769480 | tf_op jit(solution)/shard_map/ppermute | solution.py:14
  361.3 11.6 %collective-permute-start.18 = (bf16[384,3,256]{2,0,1:T(8,128)(2,1)}, bf16[384,3,256]{2,0,1:T(8,128)(2,1)}, u32[]{:S(2)}, u32[]{:S(2)}) collective-permute-start(bf16[384,3,256]{2,0,1:T(8,128)(2,1)} %slice.214), channel_id=1, source_target_pairs={{0,56},{8,64},{16,72},{24,80},{32,88},{40,96},{48,104},{56,112},{6... | collective-permute-start | bytes 1769480 | tf_op jit(solution)/shard_map/ppermute | solution.py:14
  373.0 1.9 collective-permute-start.19
  374.9 1.9 collective-permute-start.20
  376.9 1.9 collective-permute-start.21
  378.8 18.6 %collective-permute-done.17 = bf16[384,3,256]{2,0,1:T(8,128)(2,1)} collective-permute-done((bf16[384,3,256]{2,0,1:T(8,128)(2,1)}, bf16[384,3,256]{2,0,1:T(8,128)(2,1)}, u32[]{:S(2)}, u32[]{:S(2)}) %collective-permute-start.17) | collective-permute-done | bytes 589856 | tf_op jit(solution)/shard_map/ppermute | solution.py:14
  397.4 1.9 collective-permute-start.22
  399.4 31.0 %collective-permute-done.18 = bf16[384,3,256]{2,0,1:T(8,128)(2,1)} collective-permute-done((bf16[384,3,256]{2,0,1:T(8,128)(2,1)}, bf16[384,3,256]{2,0,1:T(8,128)(2,1)}, u32[]{:S(2)}, u32[]{:S(2)}) %collective-permute-start.18) | collective-permute-done | bytes 589856 | tf_op jit(solution)/shard_map/ppermute | solution.py:14
  430.4 1.9 collective-permute-start.23
  527.5 5.5 conditional.25
  533.3 8.1 %conditional.34 = ((f32[3,384]{1,0:T(4,128)}, f32[3,384]{1,0:T(4,128)S(1)}, f32[3,384,128]{2,1,0:T(8,128)S(1)})) conditional(s32[]{:T(128)} %bitcast.106, (f32[3,384]{1,0:T(4,128)}, f32[3,384]{1,0:T(4,128)S(1)}, f32[3,384,128]{2,1,0:T(8,128)S(1)}) %get-tuple-element.1021, (pred[1]{0:T(512)(128)(4,1)}, bf16[384,3,256]{2,0,1:T(8,128)(2,1)}, ...), branch_computations={%region_38.39_spmd, %region_39.42_spmd} | conditional | flops 232540416 | bytes 7447585 | solution.py:82
  541.4 5.6 conditional.35
  547.0 6.3 conditional.37
  553.3 5.6 conditional.39
  558.9 5.6 conditional.40
  564.5 6.0 conditional.41
  570.5 5.6 conditional.43
  576.1 5.6 conditional.44
  581.7 5.6 conditional.45
  587.8 2.8 convolution_convert_fusion
  590.7 59.5 %reduce-scatter.2.cloned.1.call-done = bf16[48,3072]{1,0:T(8,128)(2,1)} async-done(((bf16[384,3072]{1,0:T(8,128)(2,1)}), bf16[48,3072]{1,0:T(8,128)(2,1)}) %reduce-scatter.2.cloned.1.call-update) | async-done | bytes 294928 | tf_op jit(solution)/shard_map/reduce_scatter | solution.py:103
  (111 shorter events, 63.0 us)
Async XLA Ops:
  6.5 581.3 %copy-start = (bf16[384,3072]{1,0:T(8,128)(2,1)S(1)}, bf16[384,3072]{1,0:T(8,128)(2,1)}, u32[]{:S(2)}) copy-start(bf16[384,3072]{1,0:T(8,128)(2,1)} %param.63) | copy-start | bytes 7077892
  6.5 643.7 %reduce-scatter.2.cloned.1.call-start = ((), (), s32[]{:S(2)}) async-start(), calls=%async_computation.2 | async-start | bytes 2654208 | tf_op jit(solution)/shard_map/reduce_scatter | solution.py:103
  10.9 35.2 %copy-start.5 = (bf16[3072,3,384]{2,0,1:T(8,128)(2,1)S(1)}, bf16[3072,3,384]{2,0,1:T(8,128)(2,1)}, u32[]{:S(2)}) copy-start(bf16[3072,3,384]{2,0,1:T(8,128)(2,1)} %param.62) | copy-start | bytes 21233668
  46.1 386.3 %copy-start.2 = (s32[32]{0:T(128)S(1)}, s32[32]{0:T(128)}, u32[]{:S(2)}) copy-start(s32[32]{0:T(128)} %param.64) | copy-start | bytes 388
  46.1 389.7 %copy-start.4 = (s32[32,2]{0,1:T(2,128)S(1)}, s32[32,2]{0,1:T(2,128)}, u32[]{:S(2)}) copy-start(s32[32,2]{0,1:T(2,128)} %param.65) | copy-start | bytes 772
  49.3 0.9 copy-start.1
  51.1 34.4 %collective-permute-start = (bf16[384,3,256]{2,0,1:T(8,128)(2,1)}, bf16[384,3,256]{2,0,1:T(8,128)(2,1)}, u32[]{:S(2)}, u32[]{:S(2)}) collective-permute-start(bf16[384,3,256]{2,0,1:T(8,128)(2,1)} %slice.214), channel_id=1, source_target_pairs={{96,0},{104,8},{112,16},{120,24},{128,32},{136,40},{144,48},{152,5... | collective-permute-start | bytes 1769480 | tf_op jit(solution)/shard_map/ppermute | solution.py:14
  60.2 66.0 %collective-permute-start.1 = (bf16[384,3,256]{2,0,1:T(8,128)(2,1)}, bf16[384,3,256]{2,0,1:T(8,128)(2,1)}, u32[]{:S(2)}, u32[]{:S(2)}) collective-permute-start(bf16[384,3,256]{2,0,1:T(8,128)(2,1)} %slice.214), channel_id=1, source_target_pairs={{88,0},{96,8},{104,16},{112,24},{120,32},{128,40},{136,48},{144,56... | collective-permute-start | bytes 1769480 | tf_op jit(solution)/shard_map/ppermute | solution.py:14
  62.1 87.5 %collective-permute-start.2 = (bf16[384,3,256]{2,0,1:T(8,128)(2,1)}, bf16[384,3,256]{2,0,1:T(8,128)(2,1)}, u32[]{:S(2)}, u32[]{:S(2)}) collective-permute-start(bf16[384,3,256]{2,0,1:T(8,128)(2,1)} %slice.214), channel_id=1, source_target_pairs={{80,0},{88,8},{96,16},{104,24},{112,32},{120,40},{128,48},{136,56}... | collective-permute-start | bytes 1769480 | tf_op jit(solution)/shard_map/ppermute | solution.py:14
  64.0 100.5 %collective-permute-start.3 = (bf16[384,3,256]{2,0,1:T(8,128)(2,1)}, bf16[384,3,256]{2,0,1:T(8,128)(2,1)}, u32[]{:S(2)}, u32[]{:S(2)}) collective-permute-start(bf16[384,3,256]{2,0,1:T(8,128)(2,1)} %slice.214), channel_id=1, source_target_pairs={{72,0},{80,8},{88,16},{96,24},{104,32},{112,40},{120,48},{128,56},... | collective-permute-start | bytes 1769480 | tf_op jit(solution)/shard_map/ppermute | solution.py:14
  65.9 103.8 %collective-permute-start.4 = (bf16[384,3,256]{2,0,1:T(8,128)(2,1)}, bf16[384,3,256]{2,0,1:T(8,128)(2,1)}, u32[]{:S(2)}, u32[]{:S(2)}) collective-permute-start(bf16[384,3,256]{2,0,1:T(8,128)(2,1)} %slice.214), channel_id=1, source_target_pairs={{64,0},{72,8},{80,16},{88,24},{96,32},{104,40},{112,48},{120,56},{... | collective-permute-start | bytes 1769480 | tf_op jit(solution)/shard_map/ppermute | solution.py:14
  85.6 129.0 %collective-permute-start.5 = (bf16[384,3,256]{2,0,1:T(8,128)(2,1)}, bf16[384,3,256]{2,0,1:T(8,128)(2,1)}, u32[]{:S(2)}, u32[]{:S(2)}) collective-permute-start(bf16[384,3,256]{2,0,1:T(8,128)(2,1)} %slice.214), channel_id=1, source_target_pairs={{56,0},{64,8},{72,16},{80,24},{88,32},{96,40},{104,48},{112,56},{1... | collective-permute-start | bytes 1769480 | tf_op jit(solution)/shard_map/ppermute | solution.py:14
  126.1 90.3 %collective-permute-start.6 = (bf16[384,3,256]{2,0,1:T(8,128)(2,1)}, bf16[384,3,256]{2,0,1:T(8,128)(2,1)}, u32[]{:S(2)}, u32[]{:S(2)}) collective-permute-start(bf16[384,3,256]{2,0,1:T(8,128)(2,1)} %slice.214), channel_id=1, source_target_pairs={{48,0},{56,8},{64,16},{72,24},{80,32},{88,40},{96,48},{104,56},{11... | collective-permute-start | bytes 1769480 | tf_op jit(solution)/shard_map/ppermute | solution.py:14
  149.6 69.4 %collective-permute-start.7 = (bf16[384,3,256]{2,0,1:T(8,128)(2,1)}, bf16[384,3,256]{2,0,1:T(8,128)(2,1)}, u32[]{:S(2)}, u32[]{:S(2)}) collective-permute-start(bf16[384,3,256]{2,0,1:T(8,128)(2,1)} %slice.214), channel_id=1, source_target_pairs={{40,0},{48,8},{56,16},{64,24},{72,32},{80,40},{88,48},{96,56},{104... | collective-permute-start | bytes 1769480 | tf_op jit(solution)/shard_map/ppermute | solution.py:14
  164.5 69.2 %collective-permute-start.8 = (bf16[384,3,256]{2,0,1:T(8,128)(2,1)}, bf16[384,3,256]{2,0,1:T(8,128)(2,1)}, u32[]{:S(2)}, u32[]{:S(2)}) collective-permute-start(bf16[384,3,256]{2,0,1:T(8,128)(2,1)} %slice.214), channel_id=1, source_target_pairs={{32,0},{40,8},{48,16},{56,24},{64,32},{72,40},{80,48},{88,56},{96,... | collective-permute-start | bytes 1769480 | tf_op jit(solution)/shard_map/ppermute | solution.py:14
  169.8 87.0 %collective-permute-start.9 = (bf16[384,3,256]{2,0,1:T(8,128)(2,1)}, bf16[384,3,256]{2,0,1:T(8,128)(2,1)}, u32[]{:S(2)}, u32[]{:S(2)}) collective-permute-start(bf16[384,3,256]{2,0,1:T(8,128)(2,1)} %slice.214), channel_id=1, source_target_pairs={{24,0},{32,8},{40,16},{48,24},{56,32},{64,40},{72,48},{80,56},{88,... | collective-permute-start | bytes 1769480 | tf_op jit(solution)/shard_map/ppermute | solution.py:14
  214.5 70.0 %collective-permute-start.10 = (bf16[384,3,256]{2,0,1:T(8,128)(2,1)}, bf16[384,3,256]{2,0,1:T(8,128)(2,1)}, u32[]{:S(2)}, u32[]{:S(2)}) collective-permute-start(bf16[384,3,256]{2,0,1:T(8,128)(2,1)} %slice.214), channel_id=1, source_target_pairs={{16,0},{24,8},{32,16},{40,24},{48,32},{56,40},{64,48},{72,56},{80,... | collective-permute-start | bytes 1769480 | tf_op jit(solution)/shard_map/ppermute | solution.py:14
  216.5 112.2 %collective-permute-start.11 = (bf16[384,3,256]{2,0,1:T(8,128)(2,1)}, bf16[384,3,256]{2,0,1:T(8,128)(2,1)}, u32[]{:S(2)}, u32[]{:S(2)}) collective-permute-start(bf16[384,3,256]{2,0,1:T(8,128)(2,1)} %slice.214), channel_id=1, source_target_pairs={{8,0},{16,8},{24,16},{32,24},{40,32},{48,40},{56,48},{64,56},{72,6... | collective-permute-start | bytes 1769480 | tf_op jit(solution)/shard_map/ppermute | solution.py:14
  219.0 111.6 %collective-permute-start.12 = (bf16[384,3,256]{2,0,1:T(8,128)(2,1)}, bf16[384,3,256]{2,0,1:T(8,128)(2,1)}, u32[]{:S(2)}, u32[]{:S(2)}) collective-permute-start(bf16[384,3,256]{2,0,1:T(8,128)(2,1)} %slice.214), channel_id=1, source_target_pairs={{0,8},{8,16},{16,24},{24,32},{32,40},{40,48},{48,56},{56,64},{64,7... | collective-permute-start | bytes 1769480 | tf_op jit(solution)/shard_map/ppermute | solution.py:14
  233.6 127.7 %collective-permute-start.13 = (bf16[384,3,256]{2,0,1:T(8,128)(2,1)}, bf16[384,3,256]{2,0,1:T(8,128)(2,1)}, u32[]{:S(2)}, u32[]{:S(2)}) collective-permute-start(bf16[384,3,256]{2,0,1:T(8,128)(2,1)} %slice.214), channel_id=1, source_target_pairs={{0,16},{8,24},{16,32},{24,40},{32,48},{40,56},{48,64},{56,72},{64,... | collective-permute-start | bytes 1769480 | tf_op jit(solution)/shard_map/ppermute | solution.py:14
  256.8 116.2 %collective-permute-start.14 = (bf16[384,3,256]{2,0,1:T(8,128)(2,1)}, bf16[384,3,256]{2,0,1:T(8,128)(2,1)}, u32[]{:S(2)}, u32[]{:S(2)}) collective-permute-start(bf16[384,3,256]{2,0,1:T(8,128)(2,1)} %slice.214), channel_id=1, source_target_pairs={{0,24},{8,32},{16,40},{24,48},{32,56},{40,64},{48,72},{56,80},{64,... | collective-permute-start | bytes 1769480 | tf_op jit(solution)/shard_map/ppermute | solution.py:14
  284.5 90.4 %collective-permute-start.15 = (bf16[384,3,256]{2,0,1:T(8,128)(2,1)}, bf16[384,3,256]{2,0,1:T(8,128)(2,1)}, u32[]{:S(2)}, u32[]{:S(2)}) collective-permute-start(bf16[384,3,256]{2,0,1:T(8,128)(2,1)} %slice.214), channel_id=1, source_target_pairs={{0,32},{8,40},{16,48},{24,56},{32,64},{40,72},{48,80},{56,88},{64,... | collective-permute-start | bytes 1769480 | tf_op jit(solution)/shard_map/ppermute | solution.py:14
  328.6 48.2 %collective-permute-start.16 = (bf16[384,3,256]{2,0,1:T(8,128)(2,1)}, bf16[384,3,256]{2,0,1:T(8,128)(2,1)}, u32[]{:S(2)}, u32[]{:S(2)}) collective-permute-start(bf16[384,3,256]{2,0,1:T(8,128)(2,1)} %slice.214), channel_id=1, source_target_pairs={{0,40},{8,48},{16,56},{24,64},{32,72},{40,80},{48,88},{56,96},{64,... | collective-permute-start | bytes 1769480 | tf_op jit(solution)/shard_map/ppermute | solution.py:14
  330.6 66.9 %collective-permute-start.17 = (bf16[384,3,256]{2,0,1:T(8,128)(2,1)}, bf16[384,3,256]{2,0,1:T(8,128)(2,1)}, u32[]{:S(2)}, u32[]{:S(2)}) collective-permute-start(bf16[384,3,256]{2,0,1:T(8,128)(2,1)} %slice.214), channel_id=1, source_target_pairs={{0,48},{8,56},{16,64},{24,72},{32,80},{40,88},{48,96},{56,104},{64... | collective-permute-start | bytes 1769480 | tf_op jit(solution)/shard_map/ppermute | solution.py:14
  361.3 69.0 %collective-permute-start.18 = (bf16[384,3,256]{2,0,1:T(8,128)(2,1)}, bf16[384,3,256]{2,0,1:T(8,128)(2,1)}, u32[]{:S(2)}, u32[]{:S(2)}) collective-permute-start(bf16[384,3,256]{2,0,1:T(8,128)(2,1)} %slice.214), channel_id=1, source_target_pairs={{0,56},{8,64},{16,72},{24,80},{32,88},{40,96},{48,104},{56,112},{6... | collective-permute-start | bytes 1769480 | tf_op jit(solution)/shard_map/ppermute | solution.py:14
  373.0 208.7 %collective-permute-start.19 = (bf16[384,3,256]{2,0,1:T(8,128)(2,1)}, bf16[384,3,256]{2,0,1:T(8,128)(2,1)}, u32[]{:S(2)}, u32[]{:S(2)}) collective-permute-start(bf16[384,3,256]{2,0,1:T(8,128)(2,1)} %slice.214), channel_id=1, source_target_pairs={{0,64},{8,72},{16,80},{24,88},{32,96},{40,104},{48,112},{56,120},{... | collective-permute-start | bytes 1769480 | tf_op jit(solution)/shard_map/ppermute | solution.py:14
  374.9 212.4 %collective-permute-start.20 = (bf16[384,3,256]{2,0,1:T(8,128)(2,1)}, bf16[384,3,256]{2,0,1:T(8,128)(2,1)}, u32[]{:S(2)}, u32[]{:S(2)}) collective-permute-start(bf16[384,3,256]{2,0,1:T(8,128)(2,1)} %slice.214), channel_id=1, source_target_pairs={{0,72},{8,80},{16,88},{24,96},{32,104},{40,112},{48,120},{56,128},... | collective-permute-start | bytes 1769480 | tf_op jit(solution)/shard_map/ppermute | solution.py:14
  376.9 210.4 %collective-permute-start.21 = (bf16[384,3,256]{2,0,1:T(8,128)(2,1)}, bf16[384,3,256]{2,0,1:T(8,128)(2,1)}, u32[]{:S(2)}, u32[]{:S(2)}) collective-permute-start(bf16[384,3,256]{2,0,1:T(8,128)(2,1)} %slice.214), channel_id=1, source_target_pairs={{0,80},{8,88},{16,96},{24,104},{32,112},{40,120},{48,128},{56,136}... | collective-permute-start | bytes 1769480 | tf_op jit(solution)/shard_map/ppermute | solution.py:14
  397.4 189.9 %collective-permute-start.22 = (bf16[384,3,256]{2,0,1:T(8,128)(2,1)}, bf16[384,3,256]{2,0,1:T(8,128)(2,1)}, u32[]{:S(2)}, u32[]{:S(2)}) collective-permute-start(bf16[384,3,256]{2,0,1:T(8,128)(2,1)} %slice.214), channel_id=1, source_target_pairs={{0,88},{8,96},{16,104},{24,112},{32,120},{40,128},{48,136},{56,144... | collective-permute-start | bytes 1769480 | tf_op jit(solution)/shard_map/ppermute | solution.py:14
  430.4 157.1 %collective-permute-start.23 = (bf16[384,3,256]{2,0,1:T(8,128)(2,1)}, bf16[384,3,256]{2,0,1:T(8,128)(2,1)}, u32[]{:S(2)}, u32[]{:S(2)}) collective-permute-start(bf16[384,3,256]{2,0,1:T(8,128)(2,1)} %slice.214), channel_id=1, source_target_pairs={{0,96},{8,104},{16,112},{24,120},{32,128},{40,136},{48,144},{56,15... | collective-permute-start | bytes 1769480 | tf_op jit(solution)/shard_map/ppermute | solution.py:14
  590.7 59.6 %copy-start.3 = (f32[3072]{0:T(1024)S(1)}, f32[3072]{0:T(1024)}, u32[]{:S(2)}) copy-start(f32[3072]{0:T(1024)} %param.61) | copy-start | bytes 36868
Sparse Core Ops, SparseCore 0:
  590.8 59.3 reduce-scatter.1
